TPU v7x, 32 devices: a whole 2x2x4 slice. The times are simulated.
32 devices in a mesh: row: 4 (over z), col: 8 (over y, x, core).
Axes of the slice: x: 2, y: 2, z: 4, core: 2. Of those that a mesh axis runs over, the one named last changes fastest.
Arguments:
- factor_panel: bfloat16 [1024, 8192], P('row', 'col'), may hold values from -0.1875 to 0.1875
- ancestor_inv: float32 [1024, 1024], P('row', 'col'), may hold values from -6 to 6
- diag_inverse: float32 [4096, 8192], P('row', 'col'), may hold values from -6 to 6
- structure: int32 [2, 4], replicated, may hold values 0 or 1
Outputs:
- inverse_panel: float32 [1024, 8192], P('row', 'col')
- diag_sigma: float32 [4096, 8192], P('row', 'col')
All inputs are finite; a program needn't handle non-finite values.
Results may differ from a plain program's by a relative error of at most 0.0003.
Values may be sent and summed in bfloat16 or wider, within the bound.
A program may use at most 128 MiB of HBM per device.

v0:
```python
import jax
import jax.numpy as jnp
from jax import lax
from jax.sharding import PartitionSpec as P

B = 256
NS = 2


def local(factor_panel, ancestor_inv, diag_inverse, structure):
    rows_dev, width_dev = factor_panel.shape
    per_block = width_dev // NS
    row_index = lax.axis_index("row")
    keep_tiles = jnp.repeat(structure, B, axis=1)
    keep_own = lax.dynamic_slice_in_dim(keep_tiles, row_index * rows_dev, rows_dev, 1)
    keep_cols = jnp.repeat(keep_own.T, per_block, axis=1)
    lhat_local = jnp.where(keep_cols == 1, factor_panel, jnp.zeros_like(factor_panel))
    column = lax.all_gather(lhat_local, "row", axis=0, tiled=True)
    sigma_rows = lax.all_gather(ancestor_inv, "col", axis=1, tiled=True)
    column_wide = column.astype(jnp.float32)
    running = jnp.dot(sigma_rows, column_wide, precision=lax.Precision.HIGHEST)
    inverse_panel = jnp.where(keep_cols == 1, -running, jnp.zeros_like(running))
    rows_all = lax.all_gather(lhat_local, "col", axis=1, tiled=True)
    block_count = rows_all.shape[1] // width_dev
    rows_cube = rows_all.reshape(rows_dev, block_count, NS, per_block)
    lhat_members = [
        rows_cube[:, :, member, :].reshape(rows_dev, block_count * per_block).astype(jnp.float32)
        for member in range(NS)
    ]
    pieces = []
    for member in range(NS):
        window = lhat_members[member]
        target = inverse_panel[:, member * per_block : (member + 1) * per_block]
        pieces.append(
            lax.dot_general(
                window,
                target,
                (((0,), (0,)), ((), ())),
                precision=lax.Precision.HIGHEST,
                preferred_element_type=jnp.float32,
            )
        )
    update = lax.psum_scatter(
        jnp.concatenate(pieces, axis=1), "row", scatter_dimension=0, tiled=True
    )
    diag_sigma = diag_inverse - update
    return (inverse_panel, diag_sigma)


def solution(mesh):
    placed = (P("row", "col"), P("row", "col"), P("row", "col"), P())
    return jax.shard_map(
        local,
        mesh=mesh,
        in_specs=placed,
        out_specs=(P("row", "col"), P("row", "col")),
        check_vma=False,
    )
```

profile of v0, /device:TPU:0, one launch (start us, length us, event | category | flops | bytes accessed | tf_op | source)
XLA Modules:
  0.0 437.1 jit_solution(3430236630493984573)
XLA Ops:
  7.2 0.0 copy-start
  7.2 0.0 all-gather.6.cloned.1.call-start
  7.2 0.7 all-gather.6.cloned.1.call-update
  7.9 0.0 all-gather.4.cloned.1.call-start
  8.0 0.0 copy-done
  8.0 0.1 broadcast_bitcast_fusion
  8.1 1.2 copy.6
  9.3 0.8 bitcast_select_fusion.1
  10.2 0.0 all-gather.4.cloned.1.call-update
  10.2 0.0 all-gather.8.cloned.1.call-start
  10.2 0.7 all-gather.8.cloned.1.call-update
  10.9 0.0 reduce-scatter.2.cloned.1.call-start
  11.0 25.2 %all-gather.6.cloned.1.call-done = f32[256,1024]{1,0:T(8,128)} async-done(((f32[256,128]{1,0:T(8,128)}), f32[256,1024]{1,0:T(8,128)}) %all-gather.6.cloned.1.call-update) | async-done | bytes 1048592 | tf_op jit(solution)/shard_map/all_gather | solution.py:19
  36.2 48.4 %all-gather.4.cloned.1.call-done = bf16[1024,1024]{0,1:T(8,128)(2,1)} async-done(((bf16[256,1024]{0,1:T(8,128)(2,1)}), bf16[1024,1024]{0,1:T(8,128)(2,1)}) %all-gather.4.cloned.1.call-update) | async-done | bytes 2097168 | tf_op jit(solution)/shard_map/all_gather | solution.py:18
  84.6 3.7 bitcast_select_fusion
  88.3 33.7 %all-gather.8.cloned.1.call-done = bf16[256,8192]{0,1:T(8,128)(2,1)} async-done(((bf16[256,1024]{0,1:T(8,128)(2,1)}), bf16[256,8192]{0,1:T(8,128)(2,1)}) %all-gather.8.cloned.1.call-update) | async-done | bytes 4194320 | tf_op jit(solution)/shard_map/all_gather | solution.py:23
  122.1 2.6 fusion.5
  124.6 3.5 fusion.1
  128.1 3.5 fusion.3
  131.6 6.4 %pad_maximum_fusion = f32[4096,1024]{0,1:T(8,128)} fusion(f32[4096,512]{0,1:T(8,128)S(1)} %fusion.1, f32[4096,512]{0,1:T(8,128)S(1)} %fusion.3), kind=kLoop, calls=%fused_computation | loop fusion | flops 4194304 | bytes 33554432 | tf_op jit(solution)/shard_map/concatenate | solution.py:44
  138.0 0.0 reduce-scatter.2.cloned.1.call-update
  138.0 5.3 %copy.7 = f32[1024,1024]{0,1:T(8,128)} copy(f32[1024,1024]{1,0:T(8,128)} %param.6) | data formatting | bytes 8388608 | tf_op args[2]
  143.3 1.3 copy.8
  144.6 273.8 %reduce-scatter.2.cloned.1.call-done = f32[1024,1024]{0,1:T(8,128)} async-done(((f32[4096,1024]{0,1:T(8,128)}), f32[1024,1024]{0,1:T(8,128)}) %reduce-scatter.2.cloned.1.call-update) | async-done | bytes 4194320 | tf_op jit(solution)/shard_map/reduce_scatter | solution.py:43
  418.4 0.0 copy-start.1
  418.4 6.8 %sub.3 = f32[1024,1024]{0,1:T(8,128)} subtract(f32[1024,1024]{0,1:T(8,128)} %copy.7, f32[1024,1024]{0,1:T(8,128)} %reduce-scatter.2.cloned.1.call-done) | non-fusion elementwise | flops 1048576 | bytes 12582912 | tf_op jit(solution)/shard_map/sub | solution.py:46
  425.2 5.3 %copy.9 = f32[1024,1024]{1,0:T(8,128)} copy(f32[1024,1024]{0,1:T(8,128)} %sub.3) | data formatting | bytes 8388608
  430.6 0.0 copy-done.1
  (2 shorter events, 0.0 us)
Async XLA Ops:
  7.2 0.8 copy-start
  7.2 29.0 %all-gather.6.cloned.1.call-start = ((), (), s32[]{:S(2)}) async-start(), calls=%async_computation.2 | async-start | bytes 1179648 | tf_op jit(solution)/shard_map/all_gather | solution.py:19
  7.9 76.7 %all-gather.4.cloned.1.call-start = ((), (), s32[]{:S(2)}) async-start(), calls=%async_computation.1 | async-start | bytes 2621440 | tf_op jit(solution)/shard_map/all_gather | solution.py:18
  10.2 111.9 %all-gather.8.cloned.1.call-start = ((), (), s32[]{:S(2)}) async-start(), calls=%async_computation.3 | async-start | bytes 4718592 | tf_op jit(solution)/shard_map/all_gather | solution.py:23
  10.9 407.5 %reduce-scatter.2.cloned.1.call-start = ((), (), s32[]{:S(2)}) async-start(), calls=%async_computation.4 | async-start | bytes 20971520 | tf_op jit(solution)/shard_map/reduce_scatter | solution.py:43
  418.4 12.1 %copy-start.1 = (s32[2,4]{1,0:T(2,128)S(1)}, s32[2,4]{1,0:T(2,128)}, u32[]{:S(2)}) copy-start(s32[2,4]{1,0:T(2,128)} %param.7) | copy-start | bytes 100
Sparse Core Ops, SparseCore 0:
  9.9 26.2 all-gather.5
  38.3 46.2 all-gather.3
  87.1 34.9 all-gather.7
  138.1 280.2 reduce-scatter.1
where the time goes:
time: 437 us
  waiting for transfers between devices  383 us (88%)
  local copies, waits for them, and re-layouts  15.9 us (4%)
  other arithmetic  14 us (3%)
  between operations  13.8 us (3%)
  matrix products  10.6 us (2%)
    reduce_scatter x1, waiting for transfers between devices, local(): lax.psum_scatter(jnp.concatenate(pieces, axis=1), 'row', scatter_dimensio...  274 us
    all_gather x1, waiting for transfers between devices, local(): column = lax.all_gather(lhat_local, 'row', axis=0, tiled=True)  48.4 us
    all_gather x1, waiting for transfers between devices, local(): rows_all = lax.all_gather(lhat_local, 'col', axis=1, tiled=True)  33.7 us
    all_gather x1, waiting for transfers between devices, local(): sigma_rows = lax.all_gather(ancestor_inv, 'col', axis=1, tiled=True)  25.2 us
    unnamed x10, local copies, waits for them, and re-layouts  13.3 us
  transfers between devices with their start and end apart: 4, of which 4 were waited for; matrix products, arithmetic and copies ran while one was open for 3% of the time, Pallas kernels for 0%

commit v1 on v0

--- a/solution.py
+++ b/solution.py
@@ -16,7 +16,27 @@
     keep_cols = jnp.repeat(keep_own.T, per_block, axis=1)
     lhat_local = jnp.where(keep_cols == 1, factor_panel, jnp.zeros_like(factor_panel))
     column = lax.all_gather(lhat_local, "row", axis=0, tiled=True)
-    sigma_rows = lax.all_gather(ancestor_inv, "col", axis=1, tiled=True)
+
+    def field_view(original, in_dim):
+        carry = jax.lax.axis_size("col")
+        piece_now, w_next, all_rows = (carry, jax.lax.axis_index("col"), original.shape[in_dim])
+        a_now, moved = (original, 1)
+        while moved < piece_now:
+            a_now = jnp.concatenate(
+                [
+                    a_now,
+                    jax.lax.ppermute(
+                        a_now,
+                        "col",
+                        list(map(lambda t: (t, (t - moved) % piece_now), range(piece_now))),
+                    ),
+                ],
+                axis=in_dim,
+            )
+            moved = 2 * moved
+        return jnp.roll(a_now, w_next * all_rows, in_dim)
+
+    sigma_rows = field_view(ancestor_inv, 1)
     column_wide = column.astype(jnp.float32)
     running = jnp.dot(sigma_rows, column_wide, precision=lax.Precision.HIGHEST)
     inverse_panel = jnp.where(keep_cols == 1, -running, jnp.zeros_like(running))

time: 437 us -> 412 us (0.943)
  waiting for transfers between devices: 383 us -> 352 us
  starting transfers between devices: 0.16 us -> 4.68 us
    all_gather x1, waiting for transfers between devices: 48.4 us -> 18.8 us  [local(): column = lax.all_gather(lhat_local, 'row', axis=0, tiled=True)]
    all_gather x1 -> x0, waiting for transfers between devices: 25.2 us -> none  [local(): sigma_rows = lax.all_gather(ancestor_inv, 'col', axis=1, tiled=True)]
    ppermute x0 -> x3, waiting for transfers between devices: none -> 23.4 us  [field_view(): jax.lax.ppermute(a_now, 'col', list(map(lambda t: (t, (t - moved) % piece...]
    ppermute x0 -> x3, starting transfers between devices: none -> 4.57 us  [field_view(): jax.lax.ppermute(a_now, 'col', list(map(lambda t: (t, (t - moved) % piece...]
    unnamed x10 -> x20, local copies, waits for them, and re-layouts: 13.3 us -> 12.8 us
  transfers between devices with their start and end apart: 4 -> 6, of which waited for: 4 -> 6; matrix products, arithmetic and copies ran while one was open for 3% -> 2% of each run, Pallas kernels for 0% -> 0%
where the time goes in v1:
time: 412 us
  waiting for transfers between devices  352 us (85%)
  local copies, waits for them, and re-layouts  15.8 us (4%)
  other arithmetic  14.9 us (4%)
  between operations  13.9 us (3%)
  matrix products  10.4 us (3%)
  starting transfers between devices  4.68 us (1%)
    reduce_scatter x1, waiting for transfers between devices, local(): lax.psum_scatter(jnp.concatenate(pieces, axis=1), 'row', scatter_dimensio...  275 us
    all_gather x1, waiting for transfers between devices, local(): rows_all = lax.all_gather(lhat_local, 'col', axis=1, tiled=True)  34 us
    ppermute x3, waiting for transfers between devices, field_view(): jax.lax.ppermute(a_now, 'col', list(map(lambda t: (t, (t - moved) % piece...  23.4 us
    all_gather x1, waiting for transfers between devices, local(): column = lax.all_gather(lhat_local, 'row', axis=0, tiled=True)  18.8 us
    unnamed x20, local copies, waits for them, and re-layouts  12.8 us
  transfers between devices with their start and end apart: 6, of which 6 were waited for; matrix products, arithmetic and copies ran while one was open for 2% of the time, Pallas kernels for 0%

profile of v1, /device:TPU:0, one launch (start us, length us, event | category | flops | bytes accessed | tf_op | source)
XLA Modules:
  0.0 411.7 jit_solution(14703678888712289766)
XLA Ops:
  7.2 0.0 copy-start
  7.2 0.0 all-gather.3.cloned.1.call-start
  7.2 0.6 copy-done
  7.9 0.1 broadcast_bitcast_fusion
  7.9 1.2 copy.9
  9.2 0.8 bitcast_select_fusion
  10.0 0.0 all-gather.3.cloned.1.call-update
  10.1 0.0 all-gather.5.cloned.1.call-start
  10.1 0.7 all-gather.5.cloned.1.call-update
  10.8 0.0 reduce-scatter.2.cloned.1.call-start
  10.9 3.4 collective-permute-start
  14.3 2.5 collective-permute-done
  16.8 0.6 collective-permute-start.1
  17.4 8.1 %collective-permute-done.1 = f32[256,256]{1,0:T(8,128)S(1)} collective-permute-done((f32[256,256]{1,0:T(8,128)S(1)}, f32[256,256]{1,0:T(8,128)S(1)}, u32[]{:S(2)}, u32[]{:S(2)}) %collective-permute-start.1) | collective-permute-done | bytes 262176 | tf_op jit(solution)/shard_map/ppermute | solution.py:28
  25.5 0.9 pad_maximum_fusion.1
  26.4 0.6 collective-permute-start.2
  26.9 0.1 broadcast_in_dim.13
  27.0 0.3 copy.10
  27.4 12.8 %collective-permute-done.2 = f32[256,512]{1,0:T(8,128)S(1)} collective-permute-done((f32[256,512]{1,0:T(8,128)}, f32[256,512]{1,0:T(8,128)S(1)}, u32[]{:S(2)}, u32[]{:S(2)}) %collective-permute-start.2) | collective-permute-done | bytes 524320 | tf_op jit(solution)/shard_map/ppermute | solution.py:28
  40.4 18.8 %all-gather.3.cloned.1.call-done = bf16[1024,1024]{0,1:T(8,128)(2,1)} async-done(((bf16[256,1024]{0,1:T(8,128)(2,1)}), bf16[1024,1024]{0,1:T(8,128)(2,1)}) %all-gather.3.cloned.1.call-update) | async-done | bytes 2097168 | tf_op jit(solution)/shard_map/all_gather | solution.py:18
  59.1 3.5 fusion
  62.6 0.0 copy-start.2
  62.6 34.0 %all-gather.5.cloned.1.call-done = bf16[256,8192]{0,1:T(8,128)(2,1)} async-done(((bf16[256,1024]{0,1:T(8,128)(2,1)}), bf16[256,8192]{0,1:T(8,128)(2,1)}) %all-gather.5.cloned.1.call-update) | async-done | bytes 4194320 | tf_op jit(solution)/shard_map/all_gather | solution.py:43
  96.6 2.6 fusion.7
  99.2 3.5 fusion.2
  102.7 3.5 fusion.4
  106.2 6.4 %pad_maximum_fusion = f32[4096,1024]{0,1:T(8,128)} fusion(f32[4096,512]{0,1:T(8,128)S(1)} %fusion.2, f32[4096,512]{0,1:T(8,128)S(1)} %fusion.4), kind=kLoop, calls=%fused_computation | loop fusion | flops 4194304 | bytes 33554432 | tf_op jit(solution)/shard_map/concatenate | solution.py:64
  112.5 0.0 reduce-scatter.2.cloned.1.call-update
  112.6 5.3 %copy.13 = f32[1024,1024]{0,1:T(8,128)} copy(f32[1024,1024]{1,0:T(8,128)} %param.6) | data formatting | bytes 8388608 | tf_op args[2]
  117.9 275.1 %reduce-scatter.2.cloned.1.call-done = f32[1024,1024]{0,1:T(8,128)} async-done(((f32[4096,1024]{0,1:T(8,128)}), f32[1024,1024]{0,1:T(8,128)}) %reduce-scatter.2.cloned.1.call-update) | async-done | bytes 4194320 | tf_op jit(solution)/shard_map/reduce_scatter | solution.py:63
  393.0 6.8 %sub.8 = f32[1024,1024]{0,1:T(8,128)} subtract(f32[1024,1024]{0,1:T(8,128)} %copy.13, f32[1024,1024]{0,1:T(8,128)} %reduce-scatter.2.cloned.1.call-done) | non-fusion elementwise | flops 1048576 | bytes 12582912 | tf_op jit(solution)/shard_map/sub | solution.py:66
  399.8 5.3 %copy.14 = f32[1024,1024]{1,0:T(8,128)} copy(f32[1024,1024]{0,1:T(8,128)} %sub.8) | data formatting | bytes 8388608
  (16 shorter events, 0.2 us)
Async XLA Ops:
  7.2 0.7 copy-start
  7.2 3.7 copy-start.3
  7.2 52.0 %all-gather.3.cloned.1.call-start = ((), (), s32[]{:S(2)}) async-start(), calls=%async_computation.1 | async-start | bytes 2621440 | tf_op jit(solution)/shard_map/all_gather | solution.py:18
  10.1 86.5 %all-gather.5.cloned.1.call-start = ((), (), s32[]{:S(2)}) async-start(), calls=%async_computation.2 | async-start | bytes 4718592 | tf_op jit(solution)/shard_map/all_gather | solution.py:43
  10.8 382.2 %reduce-scatter.2.cloned.1.call-start = ((), (), s32[]{:S(2)}) async-start(), calls=%async_computation.3 | async-start | bytes 20971520 | tf_op jit(solution)/shard_map/reduce_scatter | solution.py:63
  10.9 5.9 %collective-permute-start = (f32[256,128]{1,0:T(8,128)S(1)}, f32[256,128]{1,0:T(8,128)S(1)}, u32[]{:S(2)}, u32[]{:S(2)}) collective-permute-start(f32[256,128]{1,0:T(8,128)S(1)} %copy-done.3), channel_id=1, source_target_pairs={{0,7},{1,0},{2,1},{3,2},{4,3},{5,4},{6,5},{7,6},{8,15},{9,8},{10,9... | collective-permute-start | bytes 393224 | tf_op jit(solution)/shard_map/ppermute | solution.py:28
  16.8 8.7 %collective-permute-start.1 = (f32[256,256]{1,0:T(8,128)S(1)}, f32[256,256]{1,0:T(8,128)S(1)}, u32[]{:S(2)}, u32[]{:S(2)}) collective-permute-start(f32[256,256]{1,0:T(8,128)S(1)} %pad_maximum_fusion.2), channel_id=1, source_target_pairs={{0,6},{1,7},{2,0},{3,1},{4,2},{5,3},{6,4},{7,5},{8,14},{9,15},{10,... | collective-permute-start | bytes 786440 | tf_op jit(solution)/shard_map/ppermute | solution.py:28
  26.4 13.8 %collective-permute-start.2 = (f32[256,512]{1,0:T(8,128)}, f32[256,512]{1,0:T(8,128)S(1)}, u32[]{:S(2)}, u32[]{:S(2)}) collective-permute-start(f32[256,512]{1,0:T(8,128)} %pad_maximum_fusion.1), channel_id=1, source_target_pairs={{0,4},{1,5},{2,6},{3,7},{4,0},{5,1},{6,2},{7,3},{8,12},{9,13},{10,... | collective-permute-start | bytes 1572872 | tf_op jit(solution)/shard_map/ppermute | solution.py:28
  62.6 40.1 %copy-start.2 = (f32[256,1024]{1,0:T(8,128)}, f32[256,1024]{1,0:T(8,128)S(1)}, u32[]{:S(2)}) copy-start(f32[256,1024]{1,0:T(8,128)S(1)} %fusion) | copy-start | bytes 3145732
  399.8 5.4 %copy-start.1 = (s32[2,4]{1,0:T(2,128)S(1)}, s32[2,4]{1,0:T(2,128)}, u32[]{:S(2)}) copy-start(s32[2,4]{1,0:T(2,128)} %param.7) | copy-start | bytes 100
Sparse Core Ops, SparseCore 0:
  10.2 48.9 all-gather.2
  61.6 34.9 all-gather.4
  112.7 280.2 reduce-scatter.1

commit v2 on v0

--- a/solution.py
+++ b/solution.py
@@ -15,7 +15,22 @@
     keep_own = lax.dynamic_slice_in_dim(keep_tiles, row_index * rows_dev, rows_dev, 1)
     keep_cols = jnp.repeat(keep_own.T, per_block, axis=1)
     lhat_local = jnp.where(keep_cols == 1, factor_panel, jnp.zeros_like(factor_panel))
-    column = lax.all_gather(lhat_local, "row", axis=0, tiled=True)
+    ways, here, step = (lax.axis_size("row"), lax.axis_index("row"), lhat_local.shape[0])
+    lengths = [n * ways if d == 0 else n for d, n in enumerate(lhat_local.shape)]
+    column = lax.dynamic_update_slice_in_dim(
+        jnp.zeros(lengths, lhat_local.dtype), lhat_local, here * step, axis=0
+    )
+    going_up = going_down = lhat_local
+    for far in range(1, ways // 2 + 1):
+        going_up = lax.ppermute(going_up, "row", [(d, (d + 1) % ways) for d in range(ways)])
+        column = lax.dynamic_update_slice_in_dim(
+            column, going_up, (here - far) % ways * step, axis=0
+        )
+        if 2 * far < ways:
+            going_down = lax.ppermute(going_down, "row", [(d, (d - 1) % ways) for d in range(ways)])
+            column = lax.dynamic_update_slice_in_dim(
+                column, going_down, (here + far) % ways * step, axis=0
+            )
     sigma_rows = lax.all_gather(ancestor_inv, "col", axis=1, tiled=True)
     column_wide = column.astype(jnp.float32)
     running = jnp.dot(sigma_rows, column_wide, precision=lax.Precision.HIGHEST)

time: 437 us -> 391 us (0.89)
  waiting for transfers between devices: 383 us -> 330 us
  starting transfers between devices: 0.16 us -> 5.29 us
    all_gather x1 -> x0, waiting for transfers between devices: 48.4 us -> none  [local(): column = lax.all_gather(lhat_local, 'row', axis=0, tiled=True)]
    ppermute x0 -> x3, waiting for transfers between devices: none -> 33.4 us  [the longest x2 23.3 us: local(): lax.ppermute(going_up, 'row', [(d, (d + 1) % ways) for d in range(ways)])]
    all_gather x1, waiting for transfers between devices: 25.2 us -> 0.02 us  [local(): sigma_rows = lax.all_gather(ancestor_inv, 'col', axis=1, tiled=True)]
    all_gather x1, waiting for transfers between devices: 33.7 us -> 21.9 us  [local(): rows_all = lax.all_gather(lhat_local, 'col', axis=1, tiled=True)]
    ppermute x0 -> x3, starting transfers between devices: none -> 5.17 us  [the longest x2 3.08 us: local(): lax.ppermute(going_up, 'row', [(d, (d + 1) % ways) for d in range(ways)])]
  transfers between devices with their start and end apart: 4 -> 6, of which waited for: 4 -> 5; matrix products, arithmetic and copies ran while one was open for 3% -> 3% of each run, Pallas kernels for 0% -> 0%
where the time goes in v2:
time: 391 us
  waiting for transfers between devices  330 us (84%)
  local copies, waits for them, and re-layouts  17.4 us (4%)
  other arithmetic  14 us (4%)
  between operations  13.8 us (4%)
  matrix products  10.4 us (3%)
  starting transfers between devices  5.29 us (1%)
    reduce_scatter x1, waiting for transfers between devices, local(): lax.psum_scatter(jnp.concatenate(pieces, axis=1), 'row', scatter_dimensio...  274 us
    ppermute x2, waiting for transfers between devices, local(): lax.ppermute(going_up, 'row', [(d, (d + 1) % ways) for d in range(ways)])  23.3 us
    all_gather x1, waiting for transfers between devices, local(): rows_all = lax.all_gather(lhat_local, 'col', axis=1, tiled=True)  21.9 us
    unnamed x10, local copies, waits for them, and re-layouts  13.3 us
    ppermute x1, waiting for transfers between devices, local(): lax.ppermute(going_down, 'row', [(d, (d - 1) % ways) for d in range(ways)])  10 us
  transfers between devices with their start and end apart: 6, of which 5 were waited for; matrix products, arithmetic and copies ran while one was open for 3% of the time, Pallas kernels for 0%

profile of v2, /device:TPU:0, one launch (start us, length us, event | category | flops | bytes accessed | tf_op | source)
XLA Modules:
  0.0 390.8 jit_solution(5213848980744734588)
XLA Ops:
  7.2 0.0 copy-start
  7.2 0.0 all-gather.3.cloned.1.call-start
  7.2 0.7 all-gather.3.cloned.1.call-update
  7.9 0.0 all-gather.5.cloned.1.call-start
  8.0 0.1 broadcast_bitcast_fusion
  8.1 1.2 copy.6
  9.3 0.3 broadcast_in_dim.17
  9.6 0.9 constant_dynamic-update-slice_fusion.3
  10.5 0.0 all-gather.5.cloned.1.call-update
  10.6 0.0 reduce-scatter.2.cloned.1.call-start
  10.6 3.1 collective-permute-start
  13.7 2.1 collective-permute-start.1
  15.8 12.9 %collective-permute-done = bf16[256,1024]{0,1:T(8,128)(2,1)S(1)} collective-permute-done((bf16[256,1024]{0,1:T(8,128)(2,1)}, bf16[256,1024]{0,1:T(8,128)(2,1)S(1)}, u32[]{:S(2)}, u32[]{:S(2)}) %collective-permute-start) | collective-permute-done | bytes 524320 | tf_op jit(solution)/shard_map/ppermute | solution.py:25
  28.7 0.0 collective-permute-start.2
  28.7 0.1 constant_dynamic-update-slice_fusion.2
  28.8 10.0 %collective-permute-done.1 = bf16[256,1024]{0,1:T(8,128)(2,1)} collective-permute-done((bf16[256,1024]{0,1:T(8,128)(2,1)}, bf16[256,1024]{0,1:T(8,128)(2,1)}, u32[]{:S(2)}, u32[]{:S(2)}) %collective-permute-start.1) | collective-permute-done | bytes 524320 | tf_op jit(solution)/shard_map/ppermute | solution.py:30
  38.8 1.1 constant_dynamic-update-slice_fusion.1
  39.9 10.4 %collective-permute-done.2 = bf16[256,1024]{0,1:T(8,128)(2,1)S(1)} collective-permute-done((bf16[256,1024]{0,1:T(8,128)(2,1)S(1)}, bf16[256,1024]{0,1:T(8,128)(2,1)S(1)}, u32[]{:S(2)}, u32[]{:S(2)}) %collective-permute-start.2) | collective-permute-done | bytes 524320 | tf_op jit(solution)/shard_map/ppermute | solution.py:25
  50.4 0.1 constant_dynamic-update-slice_fusion
  50.4 0.0 all-gather.3.cloned.1.call-done
  50.4 3.1 bitcast_select_fusion
  53.5 21.9 %all-gather.5.cloned.1.call-done = bf16[256,8192]{0,1:T(8,128)(2,1)} async-done(((bf16[256,1024]{0,1:T(8,128)(2,1)}), bf16[256,8192]{0,1:T(8,128)(2,1)}) %all-gather.5.cloned.1.call-update) | async-done | bytes 4194320 | tf_op jit(solution)/shard_map/all_gather | solution.py:38
  75.4 2.6 fusion.5
  78.0 3.6 fusion.3
  81.6 3.7 fusion.1
  85.3 6.3 %pad_maximum_fusion = f32[4096,1024]{0,1:T(8,128)} fusion(f32[4096,512]{0,1:T(8,128)S(1)} %fusion.1, f32[4096,512]{0,1:T(8,128)S(1)} %fusion.3), kind=kLoop, calls=%fused_computation | loop fusion | flops 4194304 | bytes 33554432 | tf_op jit(solution)/shard_map/concatenate | solution.py:59
  91.6 0.0 reduce-scatter.2.cloned.1.call-update
  91.6 5.3 %copy.7 = f32[1024,1024]{0,1:T(8,128)} copy(f32[1024,1024]{1,0:T(8,128)} %param.6) | data formatting | bytes 8388608 | tf_op args[2]
  97.0 1.3 copy.8
  98.3 273.8 %reduce-scatter.2.cloned.1.call-done = f32[1024,1024]{0,1:T(8,128)} async-done(((f32[4096,1024]{0,1:T(8,128)}), f32[1024,1024]{0,1:T(8,128)}) %reduce-scatter.2.cloned.1.call-update) | async-done | bytes 4194320 | tf_op jit(solution)/shard_map/reduce_scatter | solution.py:58
  372.1 6.8 %sub.11 = f32[1024,1024]{0,1:T(8,128)} subtract(f32[1024,1024]{0,1:T(8,128)} %copy.7, f32[1024,1024]{0,1:T(8,128)} %reduce-scatter.2.cloned.1.call-done) | non-fusion elementwise | flops 1048576 | bytes 12582912 | tf_op jit(solution)/shard_map/sub | solution.py:61
  378.9 5.3 %copy.9 = f32[1024,1024]{1,0:T(8,128)} copy(f32[1024,1024]{0,1:T(8,128)} %sub.11) | data formatting | bytes 8388608
  (5 shorter events, 0.0 us)
Async XLA Ops:
  7.2 0.8 copy-start
  7.2 43.3 %all-gather.3.cloned.1.call-start = ((), (), s32[]{:S(2)}) async-start(), calls=%async_computation.1 | async-start | bytes 1179648 | tf_op jit(solution)/shard_map/all_gather | solution.py:34
  7.9 67.5 %all-gather.5.cloned.1.call-start = ((), (), s32[]{:S(2)}) async-start(), calls=%async_computation.2 | async-start | bytes 4718592 | tf_op jit(solution)/shard_map/all_gather | solution.py:38
  10.6 361.6 %reduce-scatter.2.cloned.1.call-start = ((), (), s32[]{:S(2)}) async-start(), calls=%async_computation.3 | async-start | bytes 20971520 | tf_op jit(solution)/shard_map/reduce_scatter | solution.py:58
  10.6 18.1 %collective-permute-start = (bf16[256,1024]{0,1:T(8,128)(2,1)}, bf16[256,1024]{0,1:T(8,128)(2,1)S(1)}, u32[]{:S(2)}, u32[]{:S(2)}) collective-permute-start(bf16[256,1024]{0,1:T(8,128)(2,1)} %get-tuple-element.7), channel_id=1, source_target_pairs={{0,8},{8,16},{16,24},{24,0},{1,9},{9,17},{17,25},{25,1},{2,10},{10... | collective-permute-start | bytes 1572872 | tf_op jit(solution)/shard_map/ppermute | solution.py:25
  13.7 25.2 %collective-permute-start.1 = (bf16[256,1024]{0,1:T(8,128)(2,1)}, bf16[256,1024]{0,1:T(8,128)(2,1)}, u32[]{:S(2)}, u32[]{:S(2)}) collective-permute-start(bf16[256,1024]{0,1:T(8,128)(2,1)} %get-tuple-element.7), channel_id=1, source_target_pairs={{0,24},{8,0},{16,8},{24,16},{1,25},{9,1},{17,9},{25,17},{2,26},{10... | collective-permute-start | bytes 1572872 | tf_op jit(solution)/shard_map/ppermute | solution.py:30
  28.7 21.6 %collective-permute-start.2 = (bf16[256,1024]{0,1:T(8,128)(2,1)S(1)}, bf16[256,1024]{0,1:T(8,128)(2,1)S(1)}, u32[]{:S(2)}, u32[]{:S(2)}) collective-permute-start(bf16[256,1024]{0,1:T(8,128)(2,1)S(1)} %collective-permute-done), channel_id=1, source_target_pairs={{0,8},{8,16},{16,24},{24,0},{1,9},{9,17},{17,25},{25,1},{2,10},{10... | collective-permute-start | bytes 1572872 | tf_op jit(solution)/shard_map/ppermute | solution.py:25
  378.9 5.4 %copy-start.1 = (s32[2,4]{1,0:T(2,128)S(1)}, s32[2,4]{1,0:T(2,128)}, u32[]{:S(2)}) copy-start(s32[2,4]{1,0:T(2,128)} %param.7) | copy-start | bytes 100
Sparse Core Ops, SparseCore 0:
  9.9 26.2 all-gather.2
  38.7 36.7 all-gather.4
  91.8 280.2 reduce-scatter.1
